TPU v7x, 32 devices: a whole 2x2x4 slice. The times are simulated.
32 devices in a mesh: col: 8 (over z, x), row: 4 (over y, core).
Axes of the slice: x: 2, y: 2, z: 4, core: 2. Of those that a mesh axis runs over, the one named last changes fastest.
Arguments:
- position: float32 [128, 16384], P(None, ('col', 'row')), may hold values from -6 to 6
- momentum: float32 [128, 16384], P(None, ('col', 'row')), may hold values from -6 to 6
- row_factors: bfloat16 [16384, 16, 128], P(('col', 'row')), may hold values from -1 to 1
- col_factors: bfloat16 [16384, 16, 128], P(('col', 'row')), may hold values from -1 to 1
- tile_ranks: int32 [16, 16], replicated, may hold values from 16 to 128, as said below
- log_mean: float32 [16384], P(('col', 'row')), may hold values from -0.5 to 0.5
- counts: int32 [16384], P(('col', 'row')), may hold values from 0 to 11
- step_size: float32 [128], replicated, may hold values from 0.1 to 0.3
Outputs:
- new_position: float32 [128, 16384], P(None, ('col', 'row'))
- new_momentum: float32 [128, 16384], P(None, ('col', 'row'))
- energy_change: float32 [128], replicated
Inputs may be any that keep to these rules, and one draw needn't show every extreme that they name: `tile_ranks`: every entry is a multiple of 16; in every draw some tile has rank 16 and some tile has rank 128.
All inputs are finite; a program needn't handle non-finite values.
Results may differ from a plain program's by a relative error of at most 0.004.
Values may be sent and summed in bfloat16 or wider, within the bound.
A program may use at most 128 MiB of HBM per device.

v0:
```python
import jax
import jax.numpy as jnp
from jax import lax
from jax.sharding import PartitionSpec as P


def partner_2(value, axis, stride):
    mask = 2**stride
    pairs = [(source, source ^ mask) for source in range(lax.axis_size(axis))]
    return lax.ppermute(value, axis, pairs)


def on_device(
    position, momentum, row_factors, col_factors, tile_ranks, log_mean, counts, step_size
):
    chains = position.shape[0]
    tile_count = tile_ranks.shape[0]
    ranked = row_factors.shape[2]
    device = lax.axis_index(("col", "row"))
    own_tile = device // 2
    own_half = device % 2
    levels = jnp.arange(ranked, dtype=jnp.int32)
    col_ranks = lax.dynamic_slice_in_dim(tile_ranks, own_tile, 1, 1)[:, 0]
    row_ranks = lax.dynamic_slice_in_dim(tile_ranks, own_tile, 1, 0)[0]
    col_live = (levels[None, :] < col_ranks[:, None]).astype(jnp.float32)[:, :, None]
    row_live = (levels[None, :] < row_ranks[:, None]).astype(jnp.float32)[:, :, None]
    rate_base = counts.astype(jnp.float32)[None, :]

    def deliver(partial_value):
        halved = partial_value.reshape(2 * tile_count, ranked // 2, chains)
        arrived = lax.all_to_all(halved, ("col", "row"), split_axis=0, concat_axis=0, tiled=True)
        summed = arrived.reshape(tile_count, 2, ranked // 2, chains).astype(jnp.float32).sum(axis=1)
        summed = summed.astype(jnp.bfloat16)
        partner = partner_2(summed, "row", 0)
        lower_first = jnp.concatenate([summed, partner], axis=1)
        upper_first = jnp.concatenate([partner, summed], axis=1)
        return jnp.where(own_half == 0, lower_first, upper_first)

    def gradient(values):
        rounded = values.astype(jnp.bfloat16)
        partial_value = jnp.einsum(
            "yik,hy->ikh", col_factors, rounded, preferred_element_type=jnp.float32
        )
        partial_value = (partial_value * col_live).astype(jnp.bfloat16)
        coefficient = deliver(partial_value)
        latent_field = jnp.einsum(
            "xjk,jkh->hx", row_factors, coefficient, preferred_element_type=jnp.float32
        )
        exponent = log_mean[None, :] + latent_field
        intensity = jnp.exp(exponent)
        residual = rate_base - intensity
        adjoint = jnp.einsum(
            "xjk,hx->jkh",
            row_factors,
            residual.astype(jnp.bfloat16),
            preferred_element_type=jnp.float32,
        )
        adjoint = (adjoint * row_live).astype(jnp.bfloat16)
        returned = deliver(adjoint)
        pulled = jnp.einsum(
            "yik,ikh->hy", col_factors, returned, preferred_element_type=jnp.float32
        )
        energy = jnp.sum(intensity - rate_base * exponent + 0.5 * values * values, axis=1)
        return (values - pulled, energy)

    full_step = step_size[:, None]

    def leapfrog(section, carry):
        shifted, moment, start_energy, end_energy = carry
        forces, energy = gradient(shifted)
        weight = jnp.where(section == 1, 1.0, 0.5).astype(jnp.float32)
        moment = moment - weight * full_step * forces
        advance = jnp.where(section < 2, full_step * moment, jnp.zeros_like(moment))
        shifted = shifted + advance
        start_energy = jnp.where(section == 0, energy, start_energy)
        end_energy = jnp.where(section == 2, energy, end_energy)
        return (shifted, moment, start_energy, end_energy)

    empty = jnp.zeros((chains,), jnp.float32)
    shifted, moment, start_energy, end_energy = lax.fori_loop(
        0, 3, leapfrog, (position, momentum, empty, empty)
    )
    kinetic = 0.5 * jnp.sum(moment * moment - momentum * momentum, axis=1)
    change = lax.psum(end_energy - start_energy + kinetic, ("col", "row"))
    return (shifted, moment, change)


def solution(mesh):
    in_specs = (
        P(None, ("col", "row")),
        P(None, ("col", "row")),
        P(("col", "row"), None, None),
        P(("col", "row"), None, None),
        P(),
        P(("col", "row")),
        P(("col", "row")),
        P(),
    )
    out_specs = (P(None, ("col", "row")), P(None, ("col", "row")), P())
    return jax.shard_map(
        on_device, mesh=mesh, in_specs=in_specs, out_specs=out_specs, check_vma=False
    )
```

profile of v0, /device:TPU:0, one launch (start us, length us, event | category | flops | bytes accessed | tf_op | source)
XLA Modules:
  0.0 186.0 jit_solution(8267048132765236905)
XLA Ops:
  0.7 0.7 copy-done
  1.3 0.2 dynamic-slice_reduce_fusion
  1.5 2.1 %copy.23 = bf16[512,16,128]{2,0,1:T(8,128)(2,1)S(1)} copy(bf16[512,16,128]{2,1,0:T(8,128)(2,1)} %param.13) | data formatting | bytes 4194304
  3.7 4.4 %copy.24 = bf16[512,16,128]{0,2,1:T(8,128)(2,1)} copy(bf16[512,16,128]{2,1,0:T(8,128)(2,1)} %param.12) | data formatting | bytes 4194304
  8.2 138.8 %while.23 = (s32[]{:T(128)}, f32[128,512]{1,0:T(8,128)S(1)}, f32[128,512]{1,0:T(8,128)S(1)}, f32[128]{0:T(128)S(1)}, f32[128]{0:T(128)S(1)}, /*index=5*/f32[128,...) while((s32[]{:T(128)}, f32[128,512]{1,0:T(8,128)S(1)}, ...), condition=%wide.region_4.5_spmd.clone, body=%wide.region_0.4_spmd.clone.sunk | while | flops 1080828416 | bytes 28880336 | solution.py:80
  8.2 0.1 convert_bitcast_fusion.4
  8.3 0.9 fusion.47
  9.2 22.7 %all_to_all.30 = bf16[32,64,128]{2,1,0:T(8,128)(2,1)S(1)} all-to-all(bf16[32,64,128]{2,1,0:T(8,128)(2,1)S(1)} %bitcast.77), channel_id=1, replica_groups=mesh['col'=8,'row'=4] {'col','row'}, dimensions={0} | all-to-all | bytes 1048576 | tf_op jit(solution)/shard_map/while/body/eval_jaxpr/all_to_all | solution.py:31
  31.9 0.1 bitcast_reduce_fusion.4
  32.1 0.1 convert_bitcast_fusion.5
  32.1 1.4 collective-permute-done
  33.6 0.5 fusion.48
  34.1 0.7 fusion.49
  34.8 0.3 multiply_convert_fusion.2
  35.1 18.4 %all_to_all.31 = bf16[32,64,128]{2,1,0:T(8,128)(2,1)S(1)} all-to-all(bf16[32,64,128]{2,1,0:T(8,128)(2,1)S(1)} %bitcast.76), channel_id=1, replica_groups=mesh['col'=8,'row'=4] {'col','row'}, dimensions={0} | all-to-all | bytes 1048576 | tf_op jit(solution)/shard_map/while/body/eval_jaxpr/all_to_all | solution.py:31
  53.5 0.1 bitcast_reduce_fusion.5
  53.6 0.1 collective-permute-start.1
  53.7 1.6 collective-permute-done.1
  55.4 2.0 %fusion.50 = (f32[128]{0:T(128)S(1)}, f32[128,512]{1,0:T(8,128)S(1)}, f32[128,512]{1,0:T(8,128)S(1)}) fusion(f32[128,512]{1,0:T(8,128)S(1)} %get-tuple-element.580, f32[128,512]{1,0:T(8,128)S(1)} %fusion.48, f32[512]{0:T(512)S(1)} %bitcast.80, f32[128]{0:T(128)S(1)} %bitcast.82, pred[]{:T(512)S(6)} %lt.137, f32[128,512]{1,0:T(8,128)S(1)} %get-tuple-element.581, ...), kind=kOutput, calls=%fused_computation.29.clone.1 | convolution fusion | flops 271581056 | bytes 3935746 | tf_op jit(solution)/shard_map/while/body/eval_jaxpr/yik,ikh->hy/dot_general | solution.py:60
  57.4 0.1 convert_bitcast_fusion.4
  57.4 0.9 fusion.47
  58.3 18.4 %all_to_all.30 = bf16[32,64,128]{2,1,0:T(8,128)(2,1)S(1)} all-to-all(bf16[32,64,128]{2,1,0:T(8,128)(2,1)S(1)} %bitcast.77), channel_id=1, replica_groups=mesh['col'=8,'row'=4] {'col','row'}, dimensions={0} | all-to-all | bytes 1048576 | tf_op jit(solution)/shard_map/while/body/eval_jaxpr/all_to_all | solution.py:31
  76.7 0.1 bitcast_reduce_fusion.4
  76.9 0.1 convert_bitcast_fusion.5
  77.0 1.4 collective-permute-done
  78.4 0.5 fusion.48
  78.9 0.7 fusion.49
  79.6 0.3 multiply_convert_fusion.2
  80.0 18.4 %all_to_all.31 = bf16[32,64,128]{2,1,0:T(8,128)(2,1)S(1)} all-to-all(bf16[32,64,128]{2,1,0:T(8,128)(2,1)S(1)} %bitcast.76), channel_id=1, replica_groups=mesh['col'=8,'row'=4] {'col','row'}, dimensions={0} | all-to-all | bytes 1048576 | tf_op jit(solution)/shard_map/while/body/eval_jaxpr/all_to_all | solution.py:31
  98.4 0.1 bitcast_reduce_fusion.5
  98.4 0.1 collective-permute-start.1
  98.5 1.6 collective-permute-done.1
  100.2 1.9 %fusion.50 = (f32[128]{0:T(128)S(1)}, f32[128,512]{1,0:T(8,128)S(1)}, f32[128,512]{1,0:T(8,128)S(1)}) fusion(f32[128,512]{1,0:T(8,128)S(1)} %get-tuple-element.580, f32[128,512]{1,0:T(8,128)S(1)} %fusion.48, f32[512]{0:T(512)S(1)} %bitcast.80, f32[128]{0:T(128)S(1)} %bitcast.82, pred[]{:T(512)S(6)} %lt.137, f32[128,512]{1,0:T(8,128)S(1)} %get-tuple-element.581, ...), kind=kOutput, calls=%fused_computation.29.clone.1 | convolution fusion | flops 271581056 | bytes 3935746 | tf_op jit(solution)/shard_map/while/body/eval_jaxpr/yik,ikh->hy/dot_general | solution.py:60
  102.2 0.1 convert_bitcast_fusion.4
  102.2 0.9 fusion.47
  103.2 18.4 %all_to_all.30 = bf16[32,64,128]{2,1,0:T(8,128)(2,1)S(1)} all-to-all(bf16[32,64,128]{2,1,0:T(8,128)(2,1)S(1)} %bitcast.77), channel_id=1, replica_groups=mesh['col'=8,'row'=4] {'col','row'}, dimensions={0} | all-to-all | bytes 1048576 | tf_op jit(solution)/shard_map/while/body/eval_jaxpr/all_to_all | solution.py:31
  121.6 0.1 bitcast_reduce_fusion.4
  121.8 1.4 collective-permute-done
  123.2 0.5 fusion.48
  123.7 0.7 fusion.49
  124.4 0.3 multiply_convert_fusion.2
  124.8 18.4 %all_to_all.31 = bf16[32,64,128]{2,1,0:T(8,128)(2,1)S(1)} all-to-all(bf16[32,64,128]{2,1,0:T(8,128)(2,1)S(1)} %bitcast.76), channel_id=1, replica_groups=mesh['col'=8,'row'=4] {'col','row'}, dimensions={0} | all-to-all | bytes 1048576 | tf_op jit(solution)/shard_map/while/body/eval_jaxpr/all_to_all | solution.py:31
  143.2 0.1 bitcast_reduce_fusion.5
  143.3 0.1 collective-permute-start.1
  143.4 1.6 collective-permute-done.1
  145.0 2.0 %fusion.50 = (f32[128]{0:T(128)S(1)}, f32[128,512]{1,0:T(8,128)S(1)}, f32[128,512]{1,0:T(8,128)S(1)}) fusion(f32[128,512]{1,0:T(8,128)S(1)} %get-tuple-element.580, f32[128,512]{1,0:T(8,128)S(1)} %fusion.48, f32[512]{0:T(512)S(1)} %bitcast.80, f32[128]{0:T(128)S(1)} %bitcast.82, pred[]{:T(512)S(6)} %lt.137, f32[128,512]{1,0:T(8,128)S(1)} %get-tuple-element.581, ...), kind=kOutput, calls=%fused_computation.29.clone.1 | convolution fusion | flops 271581056 | bytes 3935746 | tf_op jit(solution)/shard_map/while/body/eval_jaxpr/yik,ikh->hy/dot_general | solution.py:60
  147.0 0.1 subtract_reduce_fusion
  147.1 38.9 %psum.7 = f32[128]{0:T(128)} all-reduce(f32[128]{0:T(128)S(1)} %multiply_add_fusion), channel_id=1, replica_groups=mesh['col'=8,'row'=4] {'col','row'}, use_global_device_ids=true, to_apply=%region_6.7 | all-reduce | flops 128 | bytes 1024 | tf_op jit(solution)/shard_map/psum | solution.py:84
  (38 shorter events, 0.4 us)
Async XLA Ops:
  0.6 0.7 copy-start
  3.7 4.4 %copy-start.7 = (s32[512]{0:T(512)S(1)}, s32[512]{0:T(512)}, u32[]{:S(2)}) copy-start(s32[512]{0:T(512)} %param.16) | copy-start | bytes 6148
  3.7 4.4 %copy-start.3 = (f32[128,512]{1,0:T(8,128)S(1)}, f32[128,512]{1,0:T(8,128)}, u32[]{:S(2)}) copy-start(f32[128,512]{1,0:T(8,128)} %param.10) | copy-start | bytes 786436
  3.7 4.4 %copy-start.6 = (f32[128,512]{1,0:T(8,128)S(1)}, f32[128,512]{1,0:T(8,128)}, u32[]{:S(2)}) copy-start(f32[128,512]{1,0:T(8,128)} %param.11) | copy-start | bytes 786436
  3.7 4.4 %copy-start.8 = (f32[512]{0:T(512)S(1)}, f32[512]{0:T(512)}, u32[]{:S(2)}) copy-start(f32[512]{0:T(512)} %param.15) | copy-start | bytes 6148
  3.7 4.4 %copy-start.9 = (f32[128]{0:T(128)S(1)}, f32[128]{0:T(128)}, u32[]{:S(2)}) copy-start(f32[128]{0:T(128)} %param.17) | copy-start | bytes 1540
  8.2 138.9 %copy-start.4 = (f32[128,512]{1,0:T(8,128)S(1)}, f32[128,512]{1,0:T(8,128)}, u32[]{:S(2)}) copy-start(f32[128,512]{1,0:T(8,128)} %param.11) | copy-start | bytes 786436
  8.3 25.4 %copy-start.1 = (bf16[512,16,128]{0,2,1:T(8,128)(2,1)S(1)}, bf16[512,16,128]{0,2,1:T(8,128)(2,1)}, u32[]{:S(2)}) copy-start(bf16[512,16,128]{0,2,1:T(8,128)(2,1)} %get-tuple-element.607) | copy-start | bytes 6291460 | tf_op jit(solution)/shard_map/while
  32.0 1.6 collective-permute-start
  53.6 1.7 collective-permute-start.1
  57.4 21.0 %copy-start.1 = (bf16[512,16,128]{0,2,1:T(8,128)(2,1)S(1)}, bf16[512,16,128]{0,2,1:T(8,128)(2,1)}, u32[]{:S(2)}) copy-start(bf16[512,16,128]{0,2,1:T(8,128)(2,1)} %get-tuple-element.607) | copy-start | bytes 6291460 | tf_op jit(solution)/shard_map/while
  76.8 1.6 collective-permute-start
  98.4 1.7 collective-permute-start.1
  102.2 21.0 %copy-start.1 = (bf16[512,16,128]{0,2,1:T(8,128)(2,1)S(1)}, bf16[512,16,128]{0,2,1:T(8,128)(2,1)}, u32[]{:S(2)}) copy-start(bf16[512,16,128]{0,2,1:T(8,128)(2,1)} %get-tuple-element.607) | copy-start | bytes 6291460 | tf_op jit(solution)/shard_map/while
  121.6 1.6 collective-permute-start
  143.3 1.7 collective-permute-start.1
  147.0 39.1 %copy-start.2 = (f32[128,512]{1,0:T(8,128)}, f32[128,512]{1,0:T(8,128)S(1)}, u32[]{:S(2)}) copy-start(f32[128,512]{1,0:T(8,128)S(1)} %get-tuple-element.347) | copy-start | bytes 786436
  147.0 39.0 %copy-start.5 = (f32[128,512]{1,0:T(8,128)}, f32[128,512]{1,0:T(8,128)S(1)}, u32[]{:S(2)}) copy-start(f32[128,512]{1,0:T(8,128)S(1)} %get-tuple-element.348) | copy-start | bytes 786436
where the time goes:
time: 187 us; the launch traced here: 186 us
  blocking collectives  154 us (82%)
  matrix products  12.1 us (6%)
  waiting for transfers between devices  9.24 us (5%)
  local copies, waits for them, and re-layouts  7.44 us (4%)
  other arithmetic  2.09 us (1%)
    all_to_all x6, blocking collectives, deliver(): lax.all_to_all(halved, ('col', 'row'), split_axis=0, concat_axis=0, tiled...  115 us
    psum x1, blocking collectives, on_device(): change = lax.psum(end_energy - start_energy + kinetic, ('col', 'row'))  38.9 us
    ppermute x6, waiting for transfers between devices, partner_2(): return lax.ppermute(value, axis, pairs)  9.24 us
    unnamed x20, local copies, waits for them, and re-layouts  7.24 us
    dot_general x3, matrix products, gradient(): jnp.einsum('yik,ikh->hy', col_factors, returned, preferred_element_type=j...  5.85 us
  transfers between devices with their start and end apart: 6, of which 6 were waited for; matrix products, arithmetic and copies ran while one was open for 0% of the time, Pallas kernels for 0%

commit v1 on v0

--- a/solution.py
+++ b/solution.py
@@ -81,7 +81,7 @@
         0, 3, leapfrog, (position, momentum, empty, empty)
     )
     kinetic = 0.5 * jnp.sum(moment * moment - momentum * momentum, axis=1)
-    change = lax.psum(end_energy - start_energy + kinetic, ("col", "row"))
+    change = lax.psum(lax.psum(end_energy - start_energy + kinetic, "row"), "col")
     return (shifted, moment, change)
 
 

time: 187 us -> 174 us (0.930)
  blocking collectives: 154 us -> 141 us
    psum x1 -> x2, blocking collectives: 38.9 us -> 26.2 us  [the longest x1 19.7 us: on_device(): lax.psum(lax.psum(end_energy - start_energy + kinetic, 'row'), 'col')]
where the time goes in v1:
time: 174 us; the launch traced here: 173 us
  blocking collectives  141 us (81%)
  matrix products  12.1 us (7%)
  waiting for transfers between devices  9.24 us (5%)
  local copies, waits for them, and re-layouts  7.44 us (4%)
  other arithmetic  2.09 us (1%)
    all_to_all x6, blocking collectives, deliver(): lax.all_to_all(halved, ('col', 'row'), split_axis=0, concat_axis=0, tiled...  115 us
    psum x1, blocking collectives, on_device(): lax.psum(lax.psum(end_energy - start_energy + kinetic, 'row'), 'col')  19.7 us
    ppermute x6, waiting for transfers between devices, partner_2(): return lax.ppermute(value, axis, pairs)  9.24 us
    unnamed x20, local copies, waits for them, and re-layouts  7.24 us
    psum x1, blocking collectives, on_device(): lax.psum(end_energy - start_energy + kinetic, 'row')  6.48 us
    dot_general x3, matrix products, gradient(): jnp.einsum('yik,ikh->hy', col_factors, returned, preferred_element_type=j...  5.85 us
  transfers between devices with their start and end apart: 6, of which 6 were waited for; matrix products, arithmetic and copies ran while one was open for 0% of the time, Pallas kernels for 0%

profile of v1, /device:TPU:0, one launch (start us, length us, event | category | flops | bytes accessed | tf_op | source)
XLA Modules:
  0.0 173.3 jit_solution(7452111277951621848)
XLA Ops:
  0.7 0.7 copy-done
  1.3 0.2 dynamic-slice_reduce_fusion
  1.5 2.1 %copy.23 = bf16[512,16,128]{2,0,1:T(8,128)(2,1)S(1)} copy(bf16[512,16,128]{2,1,0:T(8,128)(2,1)} %param.13) | data formatting | bytes 4194304
  3.7 4.4 %copy.24 = bf16[512,16,128]{0,2,1:T(8,128)(2,1)} copy(bf16[512,16,128]{2,1,0:T(8,128)(2,1)} %param.12) | data formatting | bytes 4194304
  8.2 138.8 %while.23 = (s32[]{:T(128)}, f32[128,512]{1,0:T(8,128)S(1)}, f32[128,512]{1,0:T(8,128)S(1)}, f32[128]{0:T(128)S(1)}, f32[128]{0:T(128)S(1)}, /*index=5*/f32[128,...) while((s32[]{:T(128)}, f32[128,512]{1,0:T(8,128)S(1)}, ...), condition=%wide.region_4.5_spmd.clone, body=%wide.region_0.4_spmd.clone.sunk | while | flops 1080828416 | bytes 28880336 | solution.py:80
  8.2 0.1 convert_bitcast_fusion.4
  8.3 0.9 fusion.47
  9.2 22.7 %all_to_all.30 = bf16[32,64,128]{2,1,0:T(8,128)(2,1)S(1)} all-to-all(bf16[32,64,128]{2,1,0:T(8,128)(2,1)S(1)} %bitcast.77), channel_id=1, replica_groups=mesh['col'=8,'row'=4] {'col','row'}, dimensions={0} | all-to-all | bytes 1048576 | tf_op jit(solution)/shard_map/while/body/eval_jaxpr/all_to_all | solution.py:31
  31.9 0.1 bitcast_reduce_fusion.4
  32.1 0.1 convert_bitcast_fusion.5
  32.1 1.4 collective-permute-done
  33.6 0.5 fusion.48
  34.1 0.7 fusion.49
  34.8 0.3 multiply_convert_fusion.2
  35.1 18.4 %all_to_all.31 = bf16[32,64,128]{2,1,0:T(8,128)(2,1)S(1)} all-to-all(bf16[32,64,128]{2,1,0:T(8,128)(2,1)S(1)} %bitcast.76), channel_id=1, replica_groups=mesh['col'=8,'row'=4] {'col','row'}, dimensions={0} | all-to-all | bytes 1048576 | tf_op jit(solution)/shard_map/while/body/eval_jaxpr/all_to_all | solution.py:31
  53.5 0.1 bitcast_reduce_fusion.5
  53.6 0.1 collective-permute-start.1
  53.7 1.6 collective-permute-done.1
  55.4 2.0 %fusion.50 = (f32[128]{0:T(128)S(1)}, f32[128,512]{1,0:T(8,128)S(1)}, f32[128,512]{1,0:T(8,128)S(1)}) fusion(f32[128,512]{1,0:T(8,128)S(1)} %get-tuple-element.580, f32[128,512]{1,0:T(8,128)S(1)} %fusion.48, f32[512]{0:T(512)S(1)} %bitcast.80, f32[128]{0:T(128)S(1)} %bitcast.82, pred[]{:T(512)S(6)} %lt.137, f32[128,512]{1,0:T(8,128)S(1)} %get-tuple-element.581, ...), kind=kOutput, calls=%fused_computation.29.clone.1 | convolution fusion | flops 271581056 | bytes 3935746 | tf_op jit(solution)/shard_map/while/body/eval_jaxpr/yik,ikh->hy/dot_general | solution.py:60
  57.4 0.1 convert_bitcast_fusion.4
  57.4 0.9 fusion.47
  58.3 18.4 %all_to_all.30 = bf16[32,64,128]{2,1,0:T(8,128)(2,1)S(1)} all-to-all(bf16[32,64,128]{2,1,0:T(8,128)(2,1)S(1)} %bitcast.77), channel_id=1, replica_groups=mesh['col'=8,'row'=4] {'col','row'}, dimensions={0} | all-to-all | bytes 1048576 | tf_op jit(solution)/shard_map/while/body/eval_jaxpr/all_to_all | solution.py:31
  76.7 0.1 bitcast_reduce_fusion.4
  76.9 0.1 convert_bitcast_fusion.5
  77.0 1.4 collective-permute-done
  78.4 0.5 fusion.48
  78.9 0.7 fusion.49
  79.6 0.3 multiply_convert_fusion.2
  80.0 18.4 %all_to_all.31 = bf16[32,64,128]{2,1,0:T(8,128)(2,1)S(1)} all-to-all(bf16[32,64,128]{2,1,0:T(8,128)(2,1)S(1)} %bitcast.76), channel_id=1, replica_groups=mesh['col'=8,'row'=4] {'col','row'}, dimensions={0} | all-to-all | bytes 1048576 | tf_op jit(solution)/shard_map/while/body/eval_jaxpr/all_to_all | solution.py:31
  98.4 0.1 bitcast_reduce_fusion.5
  98.4 0.1 collective-permute-start.1
  98.5 1.6 collective-permute-done.1
  100.2 1.9 %fusion.50 = (f32[128]{0:T(128)S(1)}, f32[128,512]{1,0:T(8,128)S(1)}, f32[128,512]{1,0:T(8,128)S(1)}) fusion(f32[128,512]{1,0:T(8,128)S(1)} %get-tuple-element.580, f32[128,512]{1,0:T(8,128)S(1)} %fusion.48, f32[512]{0:T(512)S(1)} %bitcast.80, f32[128]{0:T(128)S(1)} %bitcast.82, pred[]{:T(512)S(6)} %lt.137, f32[128,512]{1,0:T(8,128)S(1)} %get-tuple-element.581, ...), kind=kOutput, calls=%fused_computation.29.clone.1 | convolution fusion | flops 271581056 | bytes 3935746 | tf_op jit(solution)/shard_map/while/body/eval_jaxpr/yik,ikh->hy/dot_general | solution.py:60
  102.2 0.9 fusion.47
  103.2 18.4 %all_to_all.30 = bf16[32,64,128]{2,1,0:T(8,128)(2,1)S(1)} all-to-all(bf16[32,64,128]{2,1,0:T(8,128)(2,1)S(1)} %bitcast.77), channel_id=1, replica_groups=mesh['col'=8,'row'=4] {'col','row'}, dimensions={0} | all-to-all | bytes 1048576 | tf_op jit(solution)/shard_map/while/body/eval_jaxpr/all_to_all | solution.py:31
  121.6 0.1 bitcast_reduce_fusion.4
  121.8 1.4 collective-permute-done
  123.2 0.5 fusion.48
  123.7 0.7 fusion.49
  124.4 0.3 multiply_convert_fusion.2
  124.8 18.4 %all_to_all.31 = bf16[32,64,128]{2,1,0:T(8,128)(2,1)S(1)} all-to-all(bf16[32,64,128]{2,1,0:T(8,128)(2,1)S(1)} %bitcast.76), channel_id=1, replica_groups=mesh['col'=8,'row'=4] {'col','row'}, dimensions={0} | all-to-all | bytes 1048576 | tf_op jit(solution)/shard_map/while/body/eval_jaxpr/all_to_all | solution.py:31
  143.2 0.1 bitcast_reduce_fusion.5
  143.3 0.1 collective-permute-start.1
  143.4 1.6 collective-permute-done.1
  145.0 2.0 %fusion.50 = (f32[128]{0:T(128)S(1)}, f32[128,512]{1,0:T(8,128)S(1)}, f32[128,512]{1,0:T(8,128)S(1)}) fusion(f32[128,512]{1,0:T(8,128)S(1)} %get-tuple-element.580, f32[128,512]{1,0:T(8,128)S(1)} %fusion.48, f32[512]{0:T(512)S(1)} %bitcast.80, f32[128]{0:T(128)S(1)} %bitcast.82, pred[]{:T(512)S(6)} %lt.137, f32[128,512]{1,0:T(8,128)S(1)} %get-tuple-element.581, ...), kind=kOutput, calls=%fused_computation.29.clone.1 | convolution fusion | flops 271581056 | bytes 3935746 | tf_op jit(solution)/shard_map/while/body/eval_jaxpr/yik,ikh->hy/dot_general | solution.py:60
  147.0 0.1 subtract_reduce_fusion
  147.1 6.5 %psum.14 = f32[128]{0:T(128)S(1)} all-reduce(f32[128]{0:T(128)S(1)} %multiply_add_fusion), channel_id=1, replica_groups=mesh['col'=8,'row'=4] {'row'}, use_global_device_ids=true, to_apply=%region_6.7 | all-reduce | flops 128 | bytes 1024 | tf_op jit(solution)/shard_map/psum | solution.py:84
  153.6 19.7 %psum.15 = f32[128]{0:T(128)} all-reduce(f32[128]{0:T(128)S(1)} %psum.14), channel_id=1, replica_groups=mesh['col'=8,'row'=4] {'col'}, use_global_device_ids=true, to_apply=%region_7.8 | all-reduce | flops 128 | bytes 1024 | tf_op jit(solution)/shard_map/psum | solution.py:84
  (39 shorter events, 0.5 us)
Async XLA Ops:
  0.6 0.7 copy-start
  3.7 4.4 %copy-start.7 = (s32[512]{0:T(512)S(1)}, s32[512]{0:T(512)}, u32[]{:S(2)}) copy-start(s32[512]{0:T(512)} %param.16) | copy-start | bytes 6148
  3.7 4.4 %copy-start.3 = (f32[128,512]{1,0:T(8,128)S(1)}, f32[128,512]{1,0:T(8,128)}, u32[]{:S(2)}) copy-start(f32[128,512]{1,0:T(8,128)} %param.10) | copy-start | bytes 786436
  3.7 4.4 %copy-start.6 = (f32[128,512]{1,0:T(8,128)S(1)}, f32[128,512]{1,0:T(8,128)}, u32[]{:S(2)}) copy-start(f32[128,512]{1,0:T(8,128)} %param.11) | copy-start | bytes 786436
  3.7 4.4 %copy-start.8 = (f32[512]{0:T(512)S(1)}, f32[512]{0:T(512)}, u32[]{:S(2)}) copy-start(f32[512]{0:T(512)} %param.15) | copy-start | bytes 6148
  3.7 4.4 %copy-start.9 = (f32[128]{0:T(128)S(1)}, f32[128]{0:T(128)}, u32[]{:S(2)}) copy-start(f32[128]{0:T(128)} %param.17) | copy-start | bytes 1540
  8.2 138.9 %copy-start.4 = (f32[128,512]{1,0:T(8,128)S(1)}, f32[128,512]{1,0:T(8,128)}, u32[]{:S(2)}) copy-start(f32[128,512]{1,0:T(8,128)} %param.11) | copy-start | bytes 786436
  8.3 25.4 %copy-start.1 = (bf16[512,16,128]{0,2,1:T(8,128)(2,1)S(1)}, bf16[512,16,128]{0,2,1:T(8,128)(2,1)}, u32[]{:S(2)}) copy-start(bf16[512,16,128]{0,2,1:T(8,128)(2,1)} %get-tuple-element.607) | copy-start | bytes 6291460 | tf_op jit(solution)/shard_map/while
  32.0 1.6 collective-permute-start
  53.6 1.7 collective-permute-start.1
  57.4 21.0 %copy-start.1 = (bf16[512,16,128]{0,2,1:T(8,128)(2,1)S(1)}, bf16[512,16,128]{0,2,1:T(8,128)(2,1)}, u32[]{:S(2)}) copy-start(bf16[512,16,128]{0,2,1:T(8,128)(2,1)} %get-tuple-element.607) | copy-start | bytes 6291460 | tf_op jit(solution)/shard_map/while
  76.8 1.6 collective-permute-start
  98.4 1.7 collective-permute-start.1
  102.2 21.0 %copy-start.1 = (bf16[512,16,128]{0,2,1:T(8,128)(2,1)S(1)}, bf16[512,16,128]{0,2,1:T(8,128)(2,1)}, u32[]{:S(2)}) copy-start(bf16[512,16,128]{0,2,1:T(8,128)(2,1)} %get-tuple-element.607) | copy-start | bytes 6291460 | tf_op jit(solution)/shard_map/while
  121.6 1.6 collective-permute-start
  143.3 1.7 collective-permute-start.1
  147.0 26.3 %copy-start.2 = (f32[128,512]{1,0:T(8,128)}, f32[128,512]{1,0:T(8,128)S(1)}, u32[]{:S(2)}) copy-start(f32[128,512]{1,0:T(8,128)S(1)} %get-tuple-element.347) | copy-start | bytes 786436
  147.0 26.3 %copy-start.5 = (f32[128,512]{1,0:T(8,128)}, f32[128,512]{1,0:T(8,128)S(1)}, u32[]{:S(2)}) copy-start(f32[128,512]{1,0:T(8,128)S(1)} %get-tuple-element.348) | copy-start | bytes 786436
